TPU v7x, 32 devices: a whole 2x2x4 slice. The times are simulated.
32 devices in a mesh: child: 2 (over y), row: 4 (over x, core), col: 4 (over z).
Axes of the slice: x: 2, y: 2, z: 4, core: 2. Of those that a mesh axis runs over, the one named last changes fastest.
Arguments:
- child_blocks: float32 [2, 4096, 4096], P('child', 'row', 'col'), as said below
- child_panels: bfloat16 [2, 4096, 1024], P('child', 'row'), may hold values from -0.1875 to 0.1875
- child_patterns: int32 [2, 16, 16], replicated, may hold values from 0 to 1, as said below
- child_maps: int32 [2, 16], replicated, may hold values from 0 to 23, as said below
- parent_place: int32 [24], replicated, may hold values from 0 to 23, as said below
- parent_front: float32 [6144, 6144], P(('child', 'row'), 'col'), as said below
Outputs:
- factored: float32 [6144, 6144], P(('child', 'row'), 'col')
Inputs may be any that keep to these rules, and one draw needn't show every extreme that they name: `parent_place`: a permutation. The entries of one child are distinct; within each aligned block of 4 entries of one child, the values parent_place[child_maps[c, i]] // 6 are distinct. `child_patterns`: symmetric in its two tile dimensions, with ones on the diagonal. `child_blocks`: each child's block is symmetric. `parent_front`: symmetric; the diagonal entries inside stored tiles (parent_place[0], parent_place[0]) and (parent_place[1], parent_place[1]) lie between 200 and 400.
All inputs are finite; a program needn't handle non-finite values.
Results may differ from a plain program's by a relative error of at most 0.0003.
Values may be sent and summed in bfloat16 or wider, within the bound.
A program may use at most 128 MiB of HBM per device.

v0:
```python
import jax
import jax.numpy as jnp
from jax import lax
from jax.sharding import PartitionSpec as P

TILE = 256
PANEL = 512


def spread(block, axis, source):
    block = jnp.where(lax.axis_index(axis) == source, block, jnp.zeros_like(block))
    return lax.psum(block, axis)


def lookup(lookup_table, positions):
    matches = positions[:, None] == jnp.arange(lookup_table.shape[0], dtype=jnp.int32)[None, :]
    return jnp.sum(jnp.where(matches, lookup_table[None, :], 0), axis=1)


def find_owner(slot_list, targets):
    matches = targets[:, None] == slot_list[None, :]
    located = jnp.any(matches, axis=1)
    chosen = jnp.sum(
        jnp.where(matches, jnp.arange(slot_list.shape[0], dtype=jnp.int32)[None, :], 0), axis=1
    )
    return (located, chosen)


def select_tiles(source, located, chosen, axis_pos):
    selected = jnp.take(source, chosen, axis=axis_pos)
    dims_shape = [1] * source.ndim
    dims_shape[axis_pos] = located.shape[0]
    return jnp.where(located.reshape(dims_shape), selected, jnp.zeros((), source.dtype))


def body(child_blocks, child_panels, child_patterns, child_maps, parent_place, parent_front):
    child_index = lax.axis_index("child")
    row_index = lax.axis_index("row")
    col_index = lax.axis_index("col")
    row_count = lax.axis_size("row")
    col_count = lax.axis_size("col")
    group_count = lax.axis_size(("child", "row"))
    own_block = child_blocks[0]
    block_width = own_block.shape[0]
    tiles_dev = block_width // TILE
    rows_dev = parent_front.shape[0] // TILE
    cols_dev = parent_front.shape[1] // TILE
    own_panel = child_panels[0]
    partner = spread(own_panel, "row", col_index)
    product = lax.dot_general(
        own_panel, partner, (((1,), (1,)), ((), ())), preferred_element_type=jnp.float32
    )
    pattern = lax.dynamic_index_in_dim(child_patterns, child_index, 0, keepdims=False)
    pattern = lax.dynamic_slice(
        pattern, (row_index * tiles_dev, col_index * tiles_dev), (tiles_dev, tiles_dev)
    ).astype(jnp.float32)
    update = (own_block - product).reshape(tiles_dev, TILE, tiles_dev, TILE) * pattern[
        :, None, :, None
    ]
    slot_table = jnp.stack(
        [lookup(parent_place, child_maps[0]), lookup(parent_place, child_maps[1])]
    )
    own_slots = lax.dynamic_index_in_dim(slot_table, child_index, 0, keepdims=False)
    row_slots = lax.dynamic_slice_in_dim(own_slots, row_index * tiles_dev, tiles_dev)
    col_slots = lax.dynamic_slice_in_dim(own_slots, col_index * tiles_dev, tiles_dev)
    group_index = child_index * row_count + row_index
    row_targets = group_index * rows_dev + jnp.arange(rows_dev, dtype=jnp.int32)
    col_targets = col_index * cols_dev + jnp.arange(cols_dev, dtype=jnp.int32)
    group_ids = jnp.arange(group_count, dtype=jnp.int32)
    column_ids = jnp.arange(col_count, dtype=jnp.int32)
    located, chosen = find_owner(col_slots // cols_dev, column_ids)
    outgoing = select_tiles(update.reshape(block_width, tiles_dev, TILE), located, chosen, 1)
    incoming = lax.all_to_all(outgoing, "col", split_axis=1, concat_axis=1, tiled=True)
    located, chosen = find_owner(own_slots, col_targets)
    placed = select_tiles(incoming, located, chosen // tiles_dev, 1).reshape(
        tiles_dev, TILE, cols_dev * TILE
    )
    located, chosen = find_owner(row_slots // rows_dev, group_ids)
    outgoing_rows = select_tiles(placed, located, chosen, 0)
    incoming_rows = lax.all_to_all(
        outgoing_rows, ("child", "row"), split_axis=0, concat_axis=0, tiled=True
    )
    contribution = jnp.zeros((rows_dev, TILE, cols_dev * TILE), jnp.float32)
    for member in range(2):
        located, chosen = find_owner(slot_table[member], row_targets)
        sender = member * row_count + chosen // tiles_dev
        contribution = contribution + select_tiles(incoming_rows, located, sender, 0)
    assembled = parent_front + contribution.reshape(parent_front.shape)
    panel_slots = parent_place[0:2]
    col_local = panel_slots // cols_dev == col_index
    col_pos = panel_slots % cols_dev
    row_local = panel_slots // rows_dev == group_index
    row_pos = panel_slots % rows_dev
    front_tiles = assembled.reshape(rows_dev * TILE, cols_dev, TILE)
    column = select_tiles(front_tiles, col_local, col_pos, 1).reshape(rows_dev * TILE, PANEL)
    diagonal_part = select_tiles(
        column.reshape(rows_dev, TILE, PANEL), row_local, row_pos, 0
    ).reshape(PANEL, PANEL)
    panel_column = lax.psum(column, "col")
    diagonal_block = lax.psum(diagonal_part, ("child", "row", "col"))
    factor = jnp.linalg.cholesky(diagonal_block)
    panel_rows = lax.linalg.triangular_solve(
        factor, panel_column, left_side=False, lower=True, transpose_a=True
    )
    halves = []
    for member in range(2):
        halves.append(spread(panel_rows, ("child", "row"), 2 * col_index + member))
    panel_cols = jnp.concatenate(halves, axis=0)
    result = assembled - lax.dot_general(
        panel_rows,
        panel_cols,
        (((1,), (1,)), ((), ())),
        precision=lax.Precision.HIGHEST,
        preferred_element_type=jnp.float32,
    )
    result_tiles = result.reshape(rows_dev * TILE, cols_dev, TILE)
    tile_positions = jnp.arange(cols_dev, dtype=jnp.int32)
    for member in range(2):
        chosen_cols = jnp.logical_and(tile_positions == col_pos[member], col_local[member])
        result_tiles = jnp.where(
            chosen_cols[None, :, None],
            panel_rows[:, None, member * TILE : (member + 1) * TILE],
            result_tiles,
        )
    return result_tiles.reshape(parent_front.shape)


def solution(mesh):
    return jax.shard_map(
        body,
        mesh=mesh,
        in_specs=(
            P("child", "row", "col"),
            P("child", "row", None),
            P(),
            P(),
            P(),
            P(("child", "row"), "col"),
        ),
        out_specs=P(("child", "row"), "col"),
        check_vma=False,
    )
```

profile of v0, /device:TPU:0, one launch (start us, length us, event | category | flops | bytes accessed | tf_op | source)
XLA Modules:
  0.0 784.7 jit_solution(8666867808019406183)
XLA Ops:
  10.8 5.5 copy.61
  16.7 47.2 %all-reduce.7.cloned.1.call-done = bf16[1024,1024]{1,0:T(8,128)(2,1)} async-done(((bf16[1024,1024]{1,0:T(8,128)(2,1)}), bf16[1024,1024]{1,0:T(8,128)(2,1)}) %all-reduce.7.cloned.1.call-update) | async-done | bytes 2097168 | tf_op jit(solution)/shard_map/psum | solution.py:12
  63.9 5.2 bitcast_subtract_fusion
  76.5 5.2 select_bitcast_fusion
  87.4 92.4 %all-to-all-done = f32[1024,4,256]{0,2,1:T(8,128)} async-done(((f32[1024,4,256]{0,2,1:T(8,128)}), f32[1024,4,256]{0,2,1:T(8,128)}, u32[]{:S(2)}, u32[]{:S(2)}) %all-to-all-start) | async-done | bytes 4194336 | tf_op jit(solution)/shard_map/all_to_all | solution.py:73
  179.8 5.8 gather_fusion.1
  185.6 8.1 %gather.35 = f32[4,256,1536]{1,0,2:T(4,128)} reshape(f32[1024,6,256]{0,2,1:T(8,128)} %bitcast.115) | data formatting | bytes 12582912 | tf_op jit(solution)/shard_map/jit(_take)/gather | solution.py:30
  193.7 7.6 copy.63
  201.3 6.3 select_select_fusion.1
  207.6 8.6 %gather_fusion.2 = f32[8,256,1536]{2,1,0:T(8,128)} fusion(f32[4,256,1536]{2,1,0:T(8,128)} %select_select_fusion.1, s32[1024]{0:T(1024)S(1)} %pad_clamp_fusion.4), kind=kCustom, calls=%fused_computation.4 | custom fusion | bytes 25165856 | tf_op jit(solution)/shard_map/jit(_take)/gather | solution.py:30
  216.2 11.4 %select_select_fusion = f32[8,256,1536]{2,1,0:T(8,128)} fusion(f32[8,256,1536]{2,1,0:T(8,128)} %gather_fusion.2, pred[8]{0:T(512)(128)(4,1)S(1)} %compare_and_fusion.6, pred[8]{0:T(512)(128)(4,1)S(1)} %fusion.35), kind=kLoop, calls=%fused_computation.9 | loop fusion | flops 6291456 | bytes 25165840 | tf_op jit(solution)/shard_map/jit(_where)/select_n | solution.py:33
  227.6 5.3 all-to-all-start.1
  234.1 137.9 %all-to-all-done.1 = f32[8,256,1536]{2,1,0:T(8,128)} async-done(((f32[8,256,1536]{2,1,0:T(8,128)}), f32[8,256,1536]{2,1,0:T(8,128)}, u32[]{:S(2)}, u32[]{:S(2)}) %all-to-all-start.1) | async-done | bytes 12582944 | tf_op jit(solution)/shard_map/all_to_all | solution.py:80
  372.0 7.5 gather_fusion.5
  379.5 7.7 gather_fusion.6
  387.2 5.1 fusion
  395.5 6.0 copy.64
  401.6 6.1 copy.65
  424.9 125.9 %all-reduce.11.cloned.1.call-done = f32[512,512]{0,1:T(8,128)} async-done(((f32[512,512]{0,1:T(8,128)}), f32[512,512]{0,1:T(8,128)}) %all-reduce.11.cloned.1.call-update) | async-done | bytes 1048592 | tf_op jit(solution)/shard_map/psum | solution.py:100
  553.8 11.7 %cholesky.102 = f32[128,128]{1,0:T(8,128)S(1)} custom-call(f32[128,128]{1,0:T(8,128)S(1)} %cholesky.260), custom_call_target="Cholesky" | custom-call | tf_op jit(solution)/shard_map/jit(cholesky)/cholesky | solution.py:101
  565.6 9.8 %custom-call.30 = f32[1,128,128]{1,2,0:T(8,128)S(1)} custom-call(f32[1,128,128]{2,1,0:T(8,128)S(1)} %get-tuple-element.63), custom_call_target="InvertDiagBlocksLowerTriangular" | custom-call | tf_op jit(solution)/shard_map/jit(cholesky)/cholesky | solution.py:101
  576.0 11.7 %cholesky.213 = f32[128,128]{1,0:T(8,128)S(1)} custom-call(f32[128,128]{1,0:T(8,128)S(1)} %cholesky.264), custom_call_target="Cholesky" | custom-call | tf_op jit(solution)/shard_map/jit(cholesky)/cholesky | solution.py:101
  588.1 10.2 %custom-call.31 = f32[1,128,128]{1,2,0:T(8,128)S(1)} custom-call(f32[1,128,128]{2,1,0:T(8,128)S(1)} %get-tuple-element.61), custom_call_target="InvertDiagBlocksLowerTriangular" | custom-call | tf_op jit(solution)/shard_map/jit(cholesky)/cholesky | solution.py:101
  599.4 11.7 %cholesky.234 = f32[128,128]{1,0:T(8,128)S(1)} custom-call(f32[128,128]{1,0:T(8,128)S(1)} %cholesky.269), custom_call_target="Cholesky" | custom-call | tf_op jit(solution)/shard_map/jit(cholesky)/cholesky | solution.py:101
  611.3 9.8 %custom-call.32 = f32[1,128,128]{1,2,0:T(8,128)S(1)} custom-call(f32[1,128,128]{2,1,0:T(8,128)S(1)} %get-tuple-element.59), custom_call_target="InvertDiagBlocksLowerTriangular" | custom-call | tf_op jit(solution)/shard_map/jit(cholesky)/cholesky | solution.py:101
  621.9 11.8 %cholesky.251 = f32[128,128]{1,0:T(8,128)S(1)} custom-call(f32[128,128]{1,0:T(8,128)S(1)} %convolution_subtract_fusion.5), custom_call_target="Cholesky" | custom-call | tf_op jit(solution)/shard_map/jit(cholesky)/cholesky | solution.py:101
  639.1 8.0 %while.1 = (s32[]{:T(128)}, f32[512,512]{0,1:T(8,128)S(1)}, s32[4,2]{0,1:T(2,128)S(1)}, f32[4,128,128]{2,1,0:T(8,128)S(1)}, s32[]{:T(128)}) while((s32[]{:T(128)}, f32[512,512]{0,1:T(8,128)S(1)}, s32[4,2]{0,1:T(2,128)S(1)}, f32[4,128,128]{2,1,0:T(8,128)S(1)}, s32[]{:T(128)}) %tuple.46), condition=%wide.while_cond, body=%wide.while_body.sunk | while | flops 2 | bytes 393321 | solution.py:102
  647.0 39.3 %custom-call.33 = f32[4,128,128]{1,2,0:T(8,128)S(1)} custom-call(f32[4,128,128]{2,1,0:T(8,128)S(1)} %get-tuple-element.13), custom_call_target="InvertDiagBlocksLowerTriangular" | custom-call | tf_op jit(solution)/shard_map/triangular_solve | solution.py:102
  703.1 6.1 copy.81
  711.8 6.2 copy.82
  718.0 46.9 %all-reduce.13.cloned.1.call-done = (f32[768,512]{0,1:T(8,128)}, f32[768,512]{0,1:T(8,128)}) async-done(((f32[768,512]{0,1:T(8,128)}, f32[768,512]{0,1:T(8,128)}), (f32[768,512]{0,1:T(8,128)}, f32[768,512]{0,1:T(8,128)})) %all-reduce.13.cloned.1.call-update) | async-done | bytes 3145744 | tf_op jit(solution)/shard_map/psum | solution.py:12
  764.9 13.1 %select_select_fusion.4 = f32[768,1536]{1,0:T(8,128)} fusion(f32[768,1536]{1,0:T(8,128)} %copy.82, f32[768,1536]{1,0:T(8,128)} %copy.81, f32[768,1536]{1,0:T(8,128)} %bitcast_add_fusion, f32[768,512]{0,1:T(8,128)} %get-tuple-element.44, f32[768,512]{0,1:T(8,128)} %get-tuple-element.45, pred[1536]{0:T(1024)(128)(4,1)S(1)} %broadcast_in_dim.367, ...), kind=kOutput, calls=%fused_computation.15 | convolution fusion | flops 7253262336 | bytes 23596032 | tf_op jit(solution)/shard_map/dot_general | solution.py:109
  (154 shorter events, 75.1 us)
Async XLA Ops:
  6.5 3.1 copy-start.2
  6.5 4.1 copy-start.1
  6.5 57.3 %all-reduce.7.cloned.1.call-start = ((), (), s32[]{:S(2)}) async-start(), calls=%async_computation.2 | async-start | bytes 4194304 | tf_op jit(solution)/shard_map/psum | solution.py:12
  10.8 53.1 %copy-start = (bf16[1,1024,1024]{2,1,0:T(8,128)(2,1)S(1)}, bf16[1,1024,1024]{2,1,0:T(8,128)(2,1)}, u32[]{:S(2)}) copy-start(bf16[1,1024,1024]{2,1,0:T(8,128)(2,1)} %param.9) | copy-start | bytes 6291460
  81.7 98.1 %all-to-all-start = ((f32[1024,4,256]{0,2,1:T(8,128)}), f32[1024,4,256]{0,2,1:T(8,128)}, u32[]{:S(2)}, u32[]{:S(2)}) async-start(f32[1024,4,256]{0,2,1:T(8,128)} %select_bitcast_fusion), calls=%async_computation | async-start | bytes 8388608 | tf_op jit(solution)/shard_map/all_to_all | solution.py:73
  227.6 144.3 %all-to-all-start.1 = ((f32[8,256,1536]{2,1,0:T(8,128)}), f32[8,256,1536]{2,1,0:T(8,128)}, u32[]{:S(2)}, u32[]{:S(2)}) async-start(f32[8,256,1536]{2,1,0:T(8,128)} %select_select_fusion), calls=%async_computation.1 | async-start | bytes 25165824 | tf_op jit(solution)/shard_map/all_to_all | solution.py:80
  233.0 317.8 %all-reduce.11.cloned.1.call-start = ((), (), s32[]{:S(2)}) async-start(), calls=%async_computation.4 | async-start | bytes 2097152 | tf_op jit(solution)/shard_map/psum | solution.py:100
  379.5 12.8 %slice-start = ((s8[4718592]{0:T(1024)(128)(4,1)}), s8[524288]{0:T(1024)(128)(4,1)S(1)}, s32[]{:S(2)}) async-start(s8[4718592]{0:T(1024)(128)(4,1)} %bitcast.121), calls=%async_computation.6 | async-start | bytes 1048576
  387.2 5.1 slice-start.1
  422.7 263.7 %all-reduce.9.cloned.1.call-start = ((), (), s32[]{:S(2)}) async-start(), calls=%async_computation.3 | async-start | bytes 3145728 | tf_op jit(solution)/shard_map/psum | solution.py:99
  424.7 340.2 %all-reduce.13.cloned.1.call-start = ((), (), s32[]{:S(2)}) async-start(), calls=%async_computation.5 | async-start | bytes 6291456 | tf_op jit(solution)/shard_map/psum | solution.py:12
Sparse Core Ops, SparseCore 0:
  9.7 54.0 all-reduce.6
  422.8 127.9 all-reduce.10
  553.2 67.9 all-reduce.8
  696.6 68.2 all-reduce.12
where the time goes:
time: 793 us; the launch traced here: 785 us
  waiting for transfers between devices  450 us (57%)
  other arithmetic  169 us (21%)
  local copies, waits for them, and re-layouts  109 us (14%)
  matrix products  28.8 us (4%)
  between operations  16.3 us (2%)
  starting transfers between devices  10.7 us (1%)
    all_to_all x1, waiting for transfers between devices, body(): lax.all_to_all(outgoing_rows, ('child', 'row'), split_axis=0, concat_axis...  138 us
    psum x1, waiting for transfers between devices, body(): diagonal_block = lax.psum(diagonal_part, ('child', 'row', 'col'))  126 us
    psum x2, waiting for transfers between devices, spread(): return lax.psum(block, axis)  94.1 us
    all_to_all x1, waiting for transfers between devices, body(): lax.all_to_all(outgoing, 'col', split_axis=1, concat_axis=1, tiled=True)  92.4 us
    another operation x15, other arithmetic, body(): factor = jnp.linalg.cholesky(diagonal_block)  79.5 us
    gather x13, local copies, waits for them, and re-layouts, select_tiles(): selected = jnp.take(source, chosen, axis=axis_pos)  61.9 us
    another operation x5, other arithmetic, body(): lax.linalg.triangular_solve(factor, panel_column, left_side=False, lower=...  39.6 us
    select_n x6, other arithmetic, select_tiles(): jnp.where(located.reshape(dims_shape), selected, jnp.zeros((), source.dty...  28 us
  transfers between devices with their start and end apart: 6, of which 5 were waited for; matrix products, arithmetic and copies ran while one was open for 21% of the time, Pallas kernels for 0%

commit v1 on v0

--- a/solution.py
+++ b/solution.py
@@ -2,6 +2,7 @@
 import jax.numpy as jnp
 from jax import lax
 from jax.sharding import PartitionSpec as P
+from jax.lax import psum
 
 TILE = 256
 PANEL = 512
@@ -34,6 +35,11 @@
 
 
 def body(child_blocks, child_panels, child_patterns, child_maps, parent_place, parent_front):
+
+    def solve_the_chains(matrix):
+        oldest = psum(psum(matrix, ("row", "col")), "child")
+        return oldest
+
     child_index = lax.axis_index("child")
     row_index = lax.axis_index("row")
     col_index = lax.axis_index("col")
@@ -97,7 +103,7 @@
         column.reshape(rows_dev, TILE, PANEL), row_local, row_pos, 0
     ).reshape(PANEL, PANEL)
     panel_column = lax.psum(column, "col")
-    diagonal_block = lax.psum(diagonal_part, ("child", "row", "col"))
+    diagonal_block = solve_the_chains(diagonal_part)
     factor = jnp.linalg.cholesky(diagonal_block)
     panel_rows = lax.linalg.triangular_solve(
         factor, panel_column, left_side=False, lower=True, transpose_a=True

time: 793 us -> 799 us (level)
    psum x1 -> x2, waiting for transfers between devices: 126 us -> 130 us  [solve_the_chains(): oldest = psum(psum(matrix, ('row', 'col')), 'child')]
  transfers between devices with their start and end apart: 6 -> 7, of which waited for: 5 -> 6; matrix products, arithmetic and copies ran while one was open for 21% -> 21% of each run, Pallas kernels for 0% -> 0%
where the time goes in v1:
time: 799 us; the launch traced here: 790 us
  waiting for transfers between devices  456 us (57%)
  other arithmetic  169 us (21%)
  local copies, waits for them, and re-layouts  109 us (14%)
  matrix products  28.8 us (4%)
  between operations  16.4 us (2%)
  starting transfers between devices  10.8 us (1%)
    all_to_all x1, waiting for transfers between devices, body(): lax.all_to_all(outgoing_rows, ('child', 'row'), split_axis=0, concat_axis...  138 us
    psum x2, waiting for transfers between devices, solve_the_chains(): oldest = psum(psum(matrix, ('row', 'col')), 'child')  130 us
    psum x2, waiting for transfers between devices, spread(): return lax.psum(block, axis)  95.2 us
    all_to_all x1, waiting for transfers between devices, body(): lax.all_to_all(outgoing, 'col', split_axis=1, concat_axis=1, tiled=True)  92.4 us
    another operation x15, other arithmetic, body(): factor = jnp.linalg.cholesky(diagonal_block)  79.5 us
    gather x13, local copies, waits for them, and re-layouts, select_tiles(): selected = jnp.take(source, chosen, axis=axis_pos)  61.9 us
    another operation x5, other arithmetic, body(): lax.linalg.triangular_solve(factor, panel_column, left_side=False, lower=...  39.6 us
    select_n x6, other arithmetic, select_tiles(): jnp.where(located.reshape(dims_shape), selected, jnp.zeros((), source.dty...  28 us
  transfers between devices with their start and end apart: 7, of which 6 were waited for; matrix products, arithmetic and copies ran while one was open for 21% of the time, Pallas kernels for 0%

profile of v1, /device:TPU:0, one launch (start us, length us, event | category | flops | bytes accessed | tf_op | source)
XLA Modules:
  0.0 790.4 jit_solution(14623436149473355587)
XLA Ops:
  10.8 5.5 copy.61
  16.7 47.2 %all-reduce.8.cloned.1.call-done = bf16[1024,1024]{1,0:T(8,128)(2,1)} async-done(((bf16[1024,1024]{1,0:T(8,128)(2,1)}), bf16[1024,1024]{1,0:T(8,128)(2,1)}) %all-reduce.8.cloned.1.call-update) | async-done | bytes 2097168 | tf_op jit(solution)/shard_map/psum | solution.py:13
  63.9 5.2 bitcast_subtract_fusion
  76.5 5.2 select_bitcast_fusion
  87.4 92.4 %all-to-all-done = f32[1024,4,256]{0,2,1:T(8,128)} async-done(((f32[1024,4,256]{0,2,1:T(8,128)}), f32[1024,4,256]{0,2,1:T(8,128)}, u32[]{:S(2)}, u32[]{:S(2)}) %all-to-all-start) | async-done | bytes 4194336 | tf_op jit(solution)/shard_map/all_to_all | solution.py:79
  179.8 5.8 gather_fusion.1
  185.6 8.1 %gather.35 = f32[4,256,1536]{1,0,2:T(4,128)} reshape(f32[1024,6,256]{0,2,1:T(8,128)} %bitcast.115) | data formatting | bytes 12582912 | tf_op jit(solution)/shard_map/jit(_take)/gather | solution.py:31
  193.7 7.6 copy.63
  201.3 6.3 select_select_fusion.1
  207.6 8.6 %gather_fusion.2 = f32[8,256,1536]{2,1,0:T(8,128)} fusion(f32[4,256,1536]{2,1,0:T(8,128)} %select_select_fusion.1, s32[1024]{0:T(1024)S(1)} %pad_clamp_fusion.4), kind=kCustom, calls=%fused_computation.4 | custom fusion | bytes 25165856 | tf_op jit(solution)/shard_map/jit(_take)/gather | solution.py:31
  216.2 11.4 %select_select_fusion = f32[8,256,1536]{2,1,0:T(8,128)} fusion(f32[8,256,1536]{2,1,0:T(8,128)} %gather_fusion.2, pred[8]{0:T(512)(128)(4,1)S(1)} %compare_and_fusion.6, pred[8]{0:T(512)(128)(4,1)S(1)} %fusion.35), kind=kLoop, calls=%fused_computation.9 | loop fusion | flops 6291456 | bytes 25165840 | tf_op jit(solution)/shard_map/jit(_where)/select_n | solution.py:34
  227.6 5.3 all-to-all-start.1
  234.1 137.9 %all-to-all-done.1 = f32[8,256,1536]{2,1,0:T(8,128)} async-done(((f32[8,256,1536]{2,1,0:T(8,128)}), f32[8,256,1536]{2,1,0:T(8,128)}, u32[]{:S(2)}, u32[]{:S(2)}) %all-to-all-start.1) | async-done | bytes 12582944 | tf_op jit(solution)/shard_map/all_to_all | solution.py:86
  372.0 7.5 gather_fusion.5
  379.5 7.7 gather_fusion.6
  395.5 6.0 copy.64
  401.6 6.1 copy.65
  422.8 91.0 %all-reduce.12.cloned.1.call-done = f32[512,512]{0,1:T(8,128)} async-done(((f32[512,512]{0,1:T(8,128)}), f32[512,512]{0,1:T(8,128)}) %all-reduce.12.cloned.1.call-update) | async-done | bytes 1048592 | tf_op jit(solution)/shard_map/psum | solution.py:40
  516.1 39.3 %all-reduce.14.cloned.1.call-done = f32[512,512]{0,1:T(8,128)} async-done(((f32[512,512]{0,1:T(8,128)}), f32[512,512]{0,1:T(8,128)}) %all-reduce.14.cloned.1.call-update) | async-done | bytes 1048592 | tf_op jit(solution)/shard_map/psum | solution.py:40
  558.4 11.7 %cholesky.102 = f32[128,128]{1,0:T(8,128)S(1)} custom-call(f32[128,128]{1,0:T(8,128)S(1)} %cholesky.260), custom_call_target="Cholesky" | custom-call | tf_op jit(solution)/shard_map/jit(cholesky)/cholesky | solution.py:107
  570.1 9.8 %custom-call.30 = f32[1,128,128]{1,2,0:T(8,128)S(1)} custom-call(f32[1,128,128]{2,1,0:T(8,128)S(1)} %get-tuple-element.63), custom_call_target="InvertDiagBlocksLowerTriangular" | custom-call | tf_op jit(solution)/shard_map/jit(cholesky)/cholesky | solution.py:107
  580.6 11.7 %cholesky.213 = f32[128,128]{1,0:T(8,128)S(1)} custom-call(f32[128,128]{1,0:T(8,128)S(1)} %cholesky.264), custom_call_target="Cholesky" | custom-call | tf_op jit(solution)/shard_map/jit(cholesky)/cholesky | solution.py:107
  592.7 10.2 %custom-call.31 = f32[1,128,128]{1,2,0:T(8,128)S(1)} custom-call(f32[1,128,128]{2,1,0:T(8,128)S(1)} %get-tuple-element.61), custom_call_target="InvertDiagBlocksLowerTriangular" | custom-call | tf_op jit(solution)/shard_map/jit(cholesky)/cholesky | solution.py:107
  604.0 11.7 %cholesky.234 = f32[128,128]{1,0:T(8,128)S(1)} custom-call(f32[128,128]{1,0:T(8,128)S(1)} %cholesky.269), custom_call_target="Cholesky" | custom-call | tf_op jit(solution)/shard_map/jit(cholesky)/cholesky | solution.py:107
  615.8 9.8 %custom-call.32 = f32[1,128,128]{1,2,0:T(8,128)S(1)} custom-call(f32[1,128,128]{2,1,0:T(8,128)S(1)} %get-tuple-element.59), custom_call_target="InvertDiagBlocksLowerTriangular" | custom-call | tf_op jit(solution)/shard_map/jit(cholesky)/cholesky | solution.py:107
  626.5 11.8 %cholesky.251 = f32[128,128]{1,0:T(8,128)S(1)} custom-call(f32[128,128]{1,0:T(8,128)S(1)} %convolution_subtract_fusion.5), custom_call_target="Cholesky" | custom-call | tf_op jit(solution)/shard_map/jit(cholesky)/cholesky | solution.py:107
  643.6 8.0 %while.1 = (s32[]{:T(128)}, f32[512,512]{0,1:T(8,128)S(1)}, s32[4,2]{0,1:T(2,128)S(1)}, f32[4,128,128]{2,1,0:T(8,128)S(1)}, s32[]{:T(128)}) while((s32[]{:T(128)}, f32[512,512]{0,1:T(8,128)S(1)}, s32[4,2]{0,1:T(2,128)S(1)}, f32[4,128,128]{2,1,0:T(8,128)S(1)}, s32[]{:T(128)}) %tuple.46), condition=%wide.while_cond, body=%wide.while_body.sunk | while | flops 2 | bytes 393321 | solution.py:108
  651.6 39.3 %custom-call.33 = f32[4,128,128]{1,2,0:T(8,128)S(1)} custom-call(f32[4,128,128]{2,1,0:T(8,128)S(1)} %get-tuple-element.13), custom_call_target="InvertDiagBlocksLowerTriangular" | custom-call | tf_op jit(solution)/shard_map/triangular_solve | solution.py:108
  707.6 6.0 copy.81
  716.4 6.2 copy.82
  722.5 48.0 %all-reduce.16.cloned.1.call-done = (f32[768,512]{0,1:T(8,128)}, f32[768,512]{0,1:T(8,128)}) async-done(((f32[768,512]{0,1:T(8,128)}, f32[768,512]{0,1:T(8,128)}), (f32[768,512]{0,1:T(8,128)}, f32[768,512]{0,1:T(8,128)})) %all-reduce.16.cloned.1.call-update) | async-done | bytes 3145744 | tf_op jit(solution)/shard_map/psum | solution.py:13
  770.5 13.1 %select_select_fusion.4 = f32[768,1536]{1,0:T(8,128)} fusion(f32[768,1536]{1,0:T(8,128)} %copy.82, f32[768,1536]{1,0:T(8,128)} %copy.81, f32[768,1536]{1,0:T(8,128)} %bitcast_add_fusion, f32[768,512]{0,1:T(8,128)} %get-tuple-element.44, f32[768,512]{0,1:T(8,128)} %get-tuple-element.45, pred[1536]{0:T(1024)(128)(4,1)S(1)} %broadcast_in_dim.367, ...), kind=kOutput, calls=%fused_computation.15 | convolution fusion | flops 7253262336 | bytes 23596032 | tf_op jit(solution)/shard_map/dot_general | solution.py:115
  (157 shorter events, 80.2 us)
Async XLA Ops:
  6.5 3.1 copy-start.2
  6.5 4.1 copy-start.1
  6.5 57.3 %all-reduce.8.cloned.1.call-start = ((), (), s32[]{:S(2)}) async-start(), calls=%async_computation.2 | async-start | bytes 4194304 | tf_op jit(solution)/shard_map/psum | solution.py:13
  10.8 53.1 %copy-start = (bf16[1,1024,1024]{2,1,0:T(8,128)(2,1)S(1)}, bf16[1,1024,1024]{2,1,0:T(8,128)(2,1)}, u32[]{:S(2)}) copy-start(bf16[1,1024,1024]{2,1,0:T(8,128)(2,1)} %param.9) | copy-start | bytes 6291460
  81.7 98.1 %all-to-all-start = ((f32[1024,4,256]{0,2,1:T(8,128)}), f32[1024,4,256]{0,2,1:T(8,128)}, u32[]{:S(2)}, u32[]{:S(2)}) async-start(f32[1024,4,256]{0,2,1:T(8,128)} %select_bitcast_fusion), calls=%async_computation | async-start | bytes 8388608 | tf_op jit(solution)/shard_map/all_to_all | solution.py:79
  227.6 144.3 %all-to-all-start.1 = ((f32[8,256,1536]{2,1,0:T(8,128)}), f32[8,256,1536]{2,1,0:T(8,128)}, u32[]{:S(2)}, u32[]{:S(2)}) async-start(f32[8,256,1536]{2,1,0:T(8,128)} %select_select_fusion), calls=%async_computation.1 | async-start | bytes 25165824 | tf_op jit(solution)/shard_map/all_to_all | solution.py:86
  233.0 280.9 %all-reduce.12.cloned.1.call-start = ((), (), s32[]{:S(2)}) async-start(), calls=%async_computation.4 | async-start | bytes 2097152 | tf_op jit(solution)/shard_map/psum | solution.py:40
  379.5 12.8 %slice-start = ((s8[4718592]{0:T(1024)(128)(4,1)}), s8[524288]{0:T(1024)(128)(4,1)S(1)}, s32[]{:S(2)}) async-start(s8[4718592]{0:T(1024)(128)(4,1)} %bitcast.121), calls=%async_computation.7 | async-start | bytes 1048576
  387.2 5.1 slice-start.1
  422.7 132.6 %all-reduce.14.cloned.1.call-start = ((), (), s32[]{:S(2)}) async-start(), calls=%async_computation.5 | async-start | bytes 2097152 | tf_op jit(solution)/shard_map/psum | solution.py:40
  513.9 177.1 %all-reduce.10.cloned.1.call-start = ((), (), s32[]{:S(2)}) async-start(), calls=%async_computation.3 | async-start | bytes 3145728 | tf_op jit(solution)/shard_map/psum | solution.py:105
  515.8 254.7 %all-reduce.16.cloned.1.call-start = ((), (), s32[]{:S(2)}) async-start(), calls=%async_computation.6 | async-start | bytes 6291456 | tf_op jit(solution)/shard_map/psum | solution.py:13
Sparse Core Ops, SparseCore 0:
  9.7 54.0 all-reduce.7
  422.9 90.9 all-reduce.11
  516.1 39.1 all-reduce.13
  557.6 69.1 all-reduce.9
  701.1 69.3 all-reduce.15
